TPU v7x, 512 devices: a whole 4x8x8 slice. The times are simulated.
512 devices in a mesh: seq: 64 (over y_lo, x, z), head: 8 (over y_hi, core).
Axes of the slice: x: 4, y: 8 (y_hi: 4, y_lo: 2; y = y_hi * 2 + y_lo), z: 8, core: 2. Of those that a mesh axis runs over, the one named last changes fastest.
Arguments:
- queries: bfloat16 [16384, 3072], P(('seq', 'head')), may hold values from -6 to 6
- keys: bfloat16 [16384, 3072], P('seq', 'head'), may hold values from -6 to 6
- values: bfloat16 [16384, 3072], P('seq', 'head'), may hold values from -6 to 6
- window: int32 [64, 27], P('seq'), may hold values from -1 to 63, as said below
- out_weight: bfloat16 [3072, 6144], P('seq', 'head'), may hold values from -0.109375 to 0.109375
Outputs:
- projected: bfloat16 [16384, 6144], P('seq', 'head')
Inputs may be any that keep to these rules, and one draw needn't show every extreme that they name: Tile g lies at (g // 16, g // 4 % 4, g % 4) in a grid of 4 x 4 x 4 tiles. Entry k of window[g] is either -1 or the tile that lies (k // 9 - 1, k // 3 % 3 - 1, k % 3 - 1) steps away from g along time, height and width; it is -1 where that tile is outside the grid. Entry 13 is g itself.
All inputs are finite; a program needn't handle non-finite values.
Results may differ from a plain program's by a relative error of at most 0.0075.
Values may be sent and summed in bfloat16 or wider, within the bound.
A program may use at most 64 MiB of HBM per device.

v0:
```python
import jax
import jax.numpy as jnp
from jax import lax
from jax.sharding import PartitionSpec as P

HEAD_DIM = 128
GH = 4
GW = 4


def passed_along(array, axis, by):
    count = lax.axis_size(axis)
    pairs = [(i, i + by) for i in range(count) if 0 <= i + by < count]
    return lax.ppermute(array, axis, pairs)


def attend_block(softmax_state, queries, kv_block, live_keys):
    run_max, run_sum, run_acc = softmax_state
    factor = queries.shape[-1] ** (-0.5)
    scores = (
        jnp.einsum("qhd,khd->qhk", queries, kv_block[0], preferred_element_type=jnp.float32)
        * factor
    )
    scores = jnp.where(live_keys[None, None, :], scores, -1e30)
    new_max = jnp.maximum(run_max, jnp.max(scores, axis=-1))
    rescale = jnp.exp(run_max - new_max)
    weights = jnp.where(live_keys[None, None, :], jnp.exp(scores - new_max[:, :, None]), 0.0)
    run_sum = run_sum * rescale + jnp.sum(weights, axis=-1)
    run_acc = run_acc * rescale[:, :, None] + jnp.einsum(
        "qhk,khd->qhd",
        weights.astype(jnp.bfloat16),
        kv_block[1],
        preferred_element_type=jnp.float32,
    )
    return (new_max, run_sum, run_acc)


def local(queries, keys, values, window, out_weight):
    tok_rows = queries.shape[0]
    head_width = HEAD_DIM
    heads_all = queries.shape[1] // head_width
    local_q = lax.all_to_all(
        queries.reshape(tok_rows, heads_all, head_width),
        "head",
        split_axis=1,
        concat_axis=0,
        tiled=True,
    )
    tile_rows = local_q.shape[0]
    heads_dev = local_q.shape[1]
    live_tiles = window[0] >= 0
    kv_pair = jnp.stack(
        [
            keys.reshape(tile_rows, heads_dev, head_width),
            values.reshape(tile_rows, heads_dev, head_width),
        ]
    )
    softmax_state = (
        jnp.full((tile_rows, heads_dev), -1e30, jnp.float32),
        jnp.zeros((tile_rows, heads_dev), jnp.float32),
        jnp.zeros((tile_rows, heads_dev, head_width), jnp.float32),
    )
    seq_span = lax.axis_size("seq")
    plane_size = GH * GW

    def tile_mask(first_slot, tile_count):
        return jnp.repeat(live_tiles[first_slot : first_slot + tile_count], tile_rows)

    softmax_state = attend_block(softmax_state, local_q, kv_pair, tile_mask(13, 1))
    for slot_index in range(27):
        offset = (
            (slot_index // 9 - 1) * plane_size
            + (slot_index // 3 % 3 - 1) * GW
            + (slot_index % 3 - 1)
        )
        if slot_index != 13 and abs(offset) < seq_span:
            remote = passed_along(kv_pair, "seq", -offset)
            softmax_state = attend_block(softmax_state, local_q, remote, tile_mask(slot_index, 1))
    run_max, run_sum, run_acc = softmax_state
    finished = (run_acc / run_sum[:, :, None]).astype(jnp.bfloat16)
    finished = finished.reshape(tile_rows, heads_dev * head_width)
    all_heads = lax.all_gather(finished, "head", axis=1, tiled=True)
    projected = jnp.dot(
        all_heads,
        lax.all_gather(out_weight, "seq", axis=0, tiled=True),
        preferred_element_type=jnp.float32,
    )
    return projected.astype(jnp.bfloat16)


def solution(mesh):
    in_specs = (
        P(("seq", "head"), None),
        P("seq", "head"),
        P("seq", "head"),
        P("seq", None),
        P("seq", "head"),
    )
    out_specs = P("seq", "head")
    return jax.shard_map(local, mesh=mesh, in_specs=in_specs, out_specs=out_specs, check_vma=False)
```

profile of v0, /device:TPU:16, one launch (start us, length us, event | category | flops | bytes accessed | tf_op | source)
XLA Modules:
  0.0 854.9 jit_solution(16147548756407061988)
XLA Ops:
  16.3 9.0 %all-to-all-start = ((bf16[32,24,128]{2,0,1:T(8,128)(2,1)}), bf16[32,24,128]{2,0,1:T(8,128)(2,1)S(1)}, u32[]{:S(2)}, u32[]{:S(2)}) async-start(bf16[32,24,128]{2,0,1:T(8,128)(2,1)} %copy_bitcast_fusion), calls=%async_computation | async-start | bytes 393216 | tf_op jit(solution)/shard_map/all_to_all | solution.py:42
  27.4 5.1 all-to-all-done
  34.1 18.8 %collective-permute-done.25 = bf16[2,256,3,128]{3,1,2,0:T(8,128)(2,1)S(1)} collective-permute-done((bf16[2,256,3,128]{3,1,2,0:T(8,128)(2,1)S(1)}, bf16[2,256,3,128]{3,1,2,0:T(8,128)(2,1)S(1)}, u32[]{:S(2)}, u32[]{:S(2)}) %collective-permute-start.25) | collective-permute-done | bytes 393248 | tf_op jit(solution)/shard_map/ppermute | solution.py:14
  55.1 6.6 collective-permute-done.24
  70.6 50.1 %collective-permute-done.20 = bf16[2,256,3,128]{3,1,2,0:T(8,128)(2,1)S(1)} collective-permute-done((bf16[2,256,3,128]{3,1,2,0:T(8,128)(2,1)S(1)}, bf16[2,256,3,128]{3,1,2,0:T(8,128)(2,1)S(1)}, u32[]{:S(2)}, u32[]{:S(2)}) %collective-permute-start.20) | collective-permute-done | bytes 393248 | tf_op jit(solution)/shard_map/ppermute | solution.py:14
  127.2 44.3 %collective-permute-start.12 = (bf16[2,256,3,128]{3,1,2,0:T(8,128)(2,1)S(1)}, bf16[2,256,3,128]{3,1,2,0:T(8,128)(2,1)S(1)}, u32[]{:S(2)}, u32[]{:S(2)}) collective-permute-start(bf16[2,256,3,128]{3,1,2,0:T(8,128)(2,1)S(1)} %pad_maximum_fusion), channel_id=1, source_target_pairs={{0,8},{8,16},{16,24},{24,32},{32,40},{40,48},{48,56},{56,64},{64,7... | collective-permute-start | bytes 1179656 | tf_op jit(solution)/shard_map/ppermute | solution.py:14
  172.5 36.7 %collective-permute-start.11 = (bf16[2,256,3,128]{3,1,2,0:T(8,128)(2,1)S(1)}, bf16[2,256,3,128]{3,1,2,0:T(8,128)(2,1)S(1)}, u32[]{:S(2)}, u32[]{:S(2)}) collective-permute-start(bf16[2,256,3,128]{3,1,2,0:T(8,128)(2,1)S(1)} %pad_maximum_fusion), channel_id=1, source_target_pairs={{0,24},{8,32},{16,40},{24,48},{32,56},{40,64},{48,72},{56,80},{64,... | collective-permute-start | bytes 1179656 | tf_op jit(solution)/shard_map/ppermute | solution.py:14
  210.1 13.1 %collective-permute-done.15 = bf16[2,256,3,128]{3,1,2,0:T(8,128)(2,1)S(1)} collective-permute-done((bf16[2,256,3,128]{3,1,2,0:T(8,128)(2,1)S(1)}, bf16[2,256,3,128]{3,1,2,0:T(8,128)(2,1)S(1)}, u32[]{:S(2)}, u32[]{:S(2)}) %collective-permute-start.15) | collective-permute-done | bytes 393248 | tf_op jit(solution)/shard_map/ppermute | solution.py:14
  223.2 15.7 %collective-permute-start.10 = (bf16[2,256,3,128]{3,1,2,0:T(8,128)(2,1)S(1)}, bf16[2,256,3,128]{3,1,2,0:T(8,128)(2,1)S(1)}, u32[]{:S(2)}, u32[]{:S(2)}) collective-permute-start(bf16[2,256,3,128]{3,1,2,0:T(8,128)(2,1)S(1)} %pad_maximum_fusion), channel_id=1, source_target_pairs={{0,32},{8,40},{16,48},{24,56},{32,64},{40,72},{48,80},{56,88},{64,... | collective-permute-start | bytes 1179656 | tf_op jit(solution)/shard_map/ppermute | solution.py:14
  244.3 14.4 %collective-permute-start.7 = (bf16[2,256,3,128]{3,1,2,0:T(8,128)(2,1)S(1)}, bf16[2,256,3,128]{3,1,2,0:T(8,128)(2,1)S(1)}, u32[]{:S(2)}, u32[]{:S(2)}) collective-permute-start(bf16[2,256,3,128]{3,1,2,0:T(8,128)(2,1)S(1)} %pad_maximum_fusion), channel_id=1, source_target_pairs={{0,96},{8,104},{16,112},{24,120},{32,128},{40,136},{48,144},{56,15... | collective-permute-start | bytes 1179656 | tf_op jit(solution)/shard_map/ppermute | solution.py:14
  259.6 19.4 %collective-permute-start.6 = (bf16[2,256,3,128]{3,1,2,0:T(8,128)(2,1)S(1)}, bf16[2,256,3,128]{3,1,2,0:T(8,128)(2,1)S(1)}, u32[]{:S(2)}, u32[]{:S(2)}) collective-permute-start(bf16[2,256,3,128]{3,1,2,0:T(8,128)(2,1)S(1)} %pad_maximum_fusion), channel_id=1, source_target_pairs={{0,104},{8,112},{16,120},{24,128},{32,136},{40,144},{48,152},{56,1... | collective-permute-start | bytes 1179656 | tf_op jit(solution)/shard_map/ppermute | solution.py:14
  282.2 16.3 %collective-permute-done.9 = bf16[2,256,3,128]{3,1,2,0:T(8,128)(2,1)S(1)} collective-permute-done((bf16[2,256,3,128]{3,1,2,0:T(8,128)(2,1)S(1)}, bf16[2,256,3,128]{3,1,2,0:T(8,128)(2,1)S(1)}, u32[]{:S(2)}, u32[]{:S(2)}) %collective-permute-start.9) | collective-permute-done | bytes 393248 | tf_op jit(solution)/shard_map/ppermute | solution.py:14
  298.4 29.9 %collective-permute-start.4 = (bf16[2,256,3,128]{3,1,2,0:T(8,128)(2,1)S(1)}, bf16[2,256,3,128]{3,1,2,0:T(8,128)(2,1)S(1)}, u32[]{:S(2)}, u32[]{:S(2)}) collective-permute-start(bf16[2,256,3,128]{3,1,2,0:T(8,128)(2,1)S(1)} %pad_maximum_fusion), channel_id=1, source_target_pairs={{0,128},{8,136},{16,144},{24,152},{32,160},{40,168},{48,176},{56,1... | collective-permute-start | bytes 1179656 | tf_op jit(solution)/shard_map/ppermute | solution.py:14
  329.3 18.6 %collective-permute-start.3 = (bf16[2,256,3,128]{3,1,2,0:T(8,128)(2,1)S(1)}, bf16[2,256,3,128]{3,1,2,0:T(8,128)(2,1)S(1)}, u32[]{:S(2)}, u32[]{:S(2)}) collective-permute-start(bf16[2,256,3,128]{3,1,2,0:T(8,128)(2,1)S(1)} %pad_maximum_fusion), channel_id=1, source_target_pairs={{0,136},{8,144},{16,152},{24,160},{32,168},{40,176},{48,184},{56,1... | collective-permute-start | bytes 1179656 | tf_op jit(solution)/shard_map/ppermute | solution.py:14
  348.9 4.2 collective-permute-start.2
  354.0 10.9 %collective-permute-start.1 = (bf16[2,256,3,128]{3,1,2,0:T(8,128)(2,1)S(1)}, bf16[2,256,3,128]{3,1,2,0:T(8,128)(2,1)S(1)}, u32[]{:S(2)}, u32[]{:S(2)}) collective-permute-start(bf16[2,256,3,128]{3,1,2,0:T(8,128)(2,1)S(1)} %pad_maximum_fusion), channel_id=1, source_target_pairs={{0,160},{8,168},{16,176},{24,184},{32,192},{40,200},{48,208},{56,2... | collective-permute-start | bytes 1179656 | tf_op jit(solution)/shard_map/ppermute | solution.py:14
  365.8 9.8 %collective-permute-start = (bf16[2,256,3,128]{3,1,2,0:T(8,128)(2,1)S(1)}, bf16[2,256,3,128]{3,1,2,0:T(8,128)(2,1)S(1)}, u32[]{:S(2)}, u32[]{:S(2)}) collective-permute-start(bf16[2,256,3,128]{3,1,2,0:T(8,128)(2,1)S(1)} %pad_maximum_fusion), channel_id=1, source_target_pairs={{0,168},{8,176},{16,184},{24,192},{32,200},{40,208},{48,216},{56,2... | collective-permute-start | bytes 1179656 | tf_op jit(solution)/shard_map/ppermute | solution.py:14
  381.0 21.5 %collective-permute-done = bf16[2,256,3,128]{3,1,2,0:T(8,128)(2,1)S(1)} collective-permute-done((bf16[2,256,3,128]{3,1,2,0:T(8,128)(2,1)S(1)}, bf16[2,256,3,128]{3,1,2,0:T(8,128)(2,1)S(1)}, u32[]{:S(2)}, u32[]{:S(2)}) %collective-permute-start) | collective-permute-done | bytes 393248 | tf_op jit(solution)/shard_map/ppermute | solution.py:14
  411.0 1.7 fusion.139
  421.7 1.7 fusion.111
  446.9 2.5 fusion.108
  450.1 83.4 %all-gather.3.cloned.1.call-done = bf16[256,3072]{0,1:T(8,128)(2,1)} async-done(((bf16[256,384]{0,1:T(8,128)(2,1)}), bf16[256,3072]{0,1:T(8,128)(2,1)}) %all-gather.3.cloned.1.call-update) | async-done | bytes 1572880 | tf_op jit(solution)/shard_map/all_gather | solution.py:82
  533.6 309.5 %all-gather.5.cloned.1.call-done = bf16[3072,768]{1,0:T(8,128)(2,1)} async-done(((bf16[48,768]{1,0:T(8,128)(2,1)}), bf16[3072,768]{1,0:T(8,128)(2,1)}) %all-gather.5.cloned.1.call-update) | async-done | bytes 4718608 | tf_op jit(solution)/shard_map/all_gather | solution.py:85
  843.1 5.0 convolution_convert_fusion
  (120 shorter events, 92.8 us)
Async XLA Ops:
  10.4 51.3 %collective-permute-start.24 = (bf16[2,256,3,128]{3,1,2,0:T(8,128)(2,1)S(1)}, bf16[2,256,3,128]{3,1,2,0:T(8,128)(2,1)S(1)}, u32[]{:S(2)}, u32[]{:S(2)}) collective-permute-start(bf16[2,256,3,128]{3,1,2,0:T(8,128)(2,1)S(1)} %pad_maximum_fusion), channel_id=1, source_target_pairs={{160,0},{168,8},{176,16},{184,24},{192,32},{200,40},{208,48},{216,... | collective-permute-start | bytes 1179656 | tf_op jit(solution)/shard_map/ppermute | solution.py:14
  11.7 52.2 %collective-permute-start.23 = (bf16[2,256,3,128]{3,1,2,0:T(8,128)(2,1)S(1)}, bf16[2,256,3,128]{3,1,2,0:T(8,128)(2,1)S(1)}, u32[]{:S(2)}, u32[]{:S(2)}) collective-permute-start(bf16[2,256,3,128]{3,1,2,0:T(8,128)(2,1)S(1)} %pad_maximum_fusion), channel_id=1, source_target_pairs={{152,0},{160,8},{168,16},{176,24},{184,32},{192,40},{200,48},{208,... | collective-permute-start | bytes 1179656 | tf_op jit(solution)/shard_map/ppermute | solution.py:14
  13.0 53.2 %collective-permute-start.22 = (bf16[2,256,3,128]{3,1,2,0:T(8,128)(2,1)S(1)}, bf16[2,256,3,128]{3,1,2,0:T(8,128)(2,1)S(1)}, u32[]{:S(2)}, u32[]{:S(2)}) collective-permute-start(bf16[2,256,3,128]{3,1,2,0:T(8,128)(2,1)S(1)} %pad_maximum_fusion), channel_id=1, source_target_pairs={{136,0},{144,8},{152,16},{160,24},{168,32},{176,40},{184,48},{192,... | collective-permute-start | bytes 1179656 | tf_op jit(solution)/shard_map/ppermute | solution.py:14
  14.3 54.1 %collective-permute-start.21 = (bf16[2,256,3,128]{3,1,2,0:T(8,128)(2,1)S(1)}, bf16[2,256,3,128]{3,1,2,0:T(8,128)(2,1)S(1)}, u32[]{:S(2)}, u32[]{:S(2)}) collective-permute-start(bf16[2,256,3,128]{3,1,2,0:T(8,128)(2,1)S(1)} %pad_maximum_fusion), channel_id=1, source_target_pairs={{128,0},{136,8},{144,16},{152,24},{160,32},{168,40},{176,48},{184,... | collective-permute-start | bytes 1179656 | tf_op jit(solution)/shard_map/ppermute | solution.py:14
  25.3 508.3 %all-gather.3.cloned.1.call-start = ((), (), s32[]{:S(2)}) async-start(), calls=%async_computation.1 | async-start | bytes 1769472 | tf_op jit(solution)/shard_map/all_gather | solution.py:82
  52.9 67.8 %collective-permute-start.20 = (bf16[2,256,3,128]{3,1,2,0:T(8,128)(2,1)S(1)}, bf16[2,256,3,128]{3,1,2,0:T(8,128)(2,1)S(1)}, u32[]{:S(2)}, u32[]{:S(2)}) collective-permute-start(bf16[2,256,3,128]{3,1,2,0:T(8,128)(2,1)S(1)} %pad_maximum_fusion), channel_id=1, source_target_pairs={{120,0},{128,8},{136,16},{144,24},{152,32},{160,40},{168,48},{176,... | collective-permute-start | bytes 1179656 | tf_op jit(solution)/shard_map/ppermute | solution.py:14
  61.7 61.1 %collective-permute-start.19 = (bf16[2,256,3,128]{3,1,2,0:T(8,128)(2,1)S(1)}, bf16[2,256,3,128]{3,1,2,0:T(8,128)(2,1)S(1)}, u32[]{:S(2)}, u32[]{:S(2)}) collective-permute-start(bf16[2,256,3,128]{3,1,2,0:T(8,128)(2,1)S(1)} %pad_maximum_fusion), channel_id=1, source_target_pairs={{104,0},{112,8},{120,16},{128,24},{136,32},{144,40},{152,48},{160,... | collective-permute-start | bytes 1179656 | tf_op jit(solution)/shard_map/ppermute | solution.py:14
  63.9 61.1 %collective-permute-start.18 = (bf16[2,256,3,128]{3,1,2,0:T(8,128)(2,1)S(1)}, bf16[2,256,3,128]{3,1,2,0:T(8,128)(2,1)S(1)}, u32[]{:S(2)}, u32[]{:S(2)}) collective-permute-start(bf16[2,256,3,128]{3,1,2,0:T(8,128)(2,1)S(1)} %pad_maximum_fusion), channel_id=1, source_target_pairs={{96,0},{104,8},{112,16},{120,24},{128,32},{136,40},{144,48},{152,5... | collective-permute-start | bytes 1179656 | tf_op jit(solution)/shard_map/ppermute | solution.py:14
  66.1 61.1 %collective-permute-start.17 = (bf16[2,256,3,128]{3,1,2,0:T(8,128)(2,1)S(1)}, bf16[2,256,3,128]{3,1,2,0:T(8,128)(2,1)S(1)}, u32[]{:S(2)}, u32[]{:S(2)}) collective-permute-start(bf16[2,256,3,128]{3,1,2,0:T(8,128)(2,1)S(1)} %pad_maximum_fusion), channel_id=1, source_target_pairs={{88,0},{96,8},{104,16},{112,24},{120,32},{128,40},{136,48},{144,56... | collective-permute-start | bytes 1179656 | tf_op jit(solution)/shard_map/ppermute | solution.py:14
  68.4 104.2 %collective-permute-start.16 = (bf16[2,256,3,128]{3,1,2,0:T(8,128)(2,1)S(1)}, bf16[2,256,3,128]{3,1,2,0:T(8,128)(2,1)S(1)}, u32[]{:S(2)}, u32[]{:S(2)}) collective-permute-start(bf16[2,256,3,128]{3,1,2,0:T(8,128)(2,1)S(1)} %pad_maximum_fusion), channel_id=1, source_target_pairs={{40,0},{48,8},{56,16},{64,24},{72,32},{80,40},{88,48},{96,56},{104... | collective-permute-start | bytes 1179656 | tf_op jit(solution)/shard_map/ppermute | solution.py:14
  120.7 102.5 %collective-permute-start.15 = (bf16[2,256,3,128]{3,1,2,0:T(8,128)(2,1)S(1)}, bf16[2,256,3,128]{3,1,2,0:T(8,128)(2,1)S(1)}, u32[]{:S(2)}, u32[]{:S(2)}) collective-permute-start(bf16[2,256,3,128]{3,1,2,0:T(8,128)(2,1)S(1)} %pad_maximum_fusion), channel_id=1, source_target_pairs={{32,0},{40,8},{48,16},{56,24},{64,32},{72,40},{80,48},{88,56},{96,... | collective-permute-start | bytes 1179656 | tf_op jit(solution)/shard_map/ppermute | solution.py:14
  122.8 117.0 %collective-permute-start.14 = (bf16[2,256,3,128]{3,1,2,0:T(8,128)(2,1)S(1)}, bf16[2,256,3,128]{3,1,2,0:T(8,128)(2,1)S(1)}, u32[]{:S(2)}, u32[]{:S(2)}) collective-permute-start(bf16[2,256,3,128]{3,1,2,0:T(8,128)(2,1)S(1)} %pad_maximum_fusion), channel_id=1, source_target_pairs={{24,0},{32,8},{40,16},{48,24},{56,32},{64,40},{72,48},{80,56},{88,... | collective-permute-start | bytes 1179656 | tf_op jit(solution)/shard_map/ppermute | solution.py:14
  125.0 117.1 %collective-permute-start.13 = (bf16[2,256,3,128]{3,1,2,0:T(8,128)(2,1)S(1)}, bf16[2,256,3,128]{3,1,2,0:T(8,128)(2,1)S(1)}, u32[]{:S(2)}, u32[]{:S(2)}) collective-permute-start(bf16[2,256,3,128]{3,1,2,0:T(8,128)(2,1)S(1)} %pad_maximum_fusion), channel_id=1, source_target_pairs={{8,0},{16,8},{24,16},{32,24},{40,32},{48,40},{56,48},{64,56},{72,6... | collective-permute-start | bytes 1179656 | tf_op jit(solution)/shard_map/ppermute | solution.py:14
  127.2 117.1 %collective-permute-start.12 = (bf16[2,256,3,128]{3,1,2,0:T(8,128)(2,1)S(1)}, bf16[2,256,3,128]{3,1,2,0:T(8,128)(2,1)S(1)}, u32[]{:S(2)}, u32[]{:S(2)}) collective-permute-start(bf16[2,256,3,128]{3,1,2,0:T(8,128)(2,1)S(1)} %pad_maximum_fusion), channel_id=1, source_target_pairs={{0,8},{8,16},{16,24},{24,32},{32,40},{40,48},{48,56},{56,64},{64,7... | collective-permute-start | bytes 1179656 | tf_op jit(solution)/shard_map/ppermute | solution.py:14
  172.5 87.1 %collective-permute-start.11 = (bf16[2,256,3,128]{3,1,2,0:T(8,128)(2,1)S(1)}, bf16[2,256,3,128]{3,1,2,0:T(8,128)(2,1)S(1)}, u32[]{:S(2)}, u32[]{:S(2)}) collective-permute-start(bf16[2,256,3,128]{3,1,2,0:T(8,128)(2,1)S(1)} %pad_maximum_fusion), channel_id=1, source_target_pairs={{0,24},{8,32},{16,40},{24,48},{32,56},{40,64},{48,72},{56,80},{64,... | collective-permute-start | bytes 1179656 | tf_op jit(solution)/shard_map/ppermute | solution.py:14
  223.2 56.8 %collective-permute-start.10 = (bf16[2,256,3,128]{3,1,2,0:T(8,128)(2,1)S(1)}, bf16[2,256,3,128]{3,1,2,0:T(8,128)(2,1)S(1)}, u32[]{:S(2)}, u32[]{:S(2)}) collective-permute-start(bf16[2,256,3,128]{3,1,2,0:T(8,128)(2,1)S(1)} %pad_maximum_fusion), channel_id=1, source_target_pairs={{0,32},{8,40},{16,48},{24,56},{32,64},{40,72},{48,80},{56,88},{64,... | collective-permute-start | bytes 1179656 | tf_op jit(solution)/shard_map/ppermute | solution.py:14
  239.8 58.6 %collective-permute-start.9 = (bf16[2,256,3,128]{3,1,2,0:T(8,128)(2,1)S(1)}, bf16[2,256,3,128]{3,1,2,0:T(8,128)(2,1)S(1)}, u32[]{:S(2)}, u32[]{:S(2)}) collective-permute-start(bf16[2,256,3,128]{3,1,2,0:T(8,128)(2,1)S(1)} %pad_maximum_fusion), channel_id=1, source_target_pairs={{0,40},{8,48},{16,56},{24,64},{32,72},{40,80},{48,88},{56,96},{64,... | collective-permute-start | bytes 1179656 | tf_op jit(solution)/shard_map/ppermute | solution.py:14
  242.2 87.1 %collective-permute-start.8 = (bf16[2,256,3,128]{3,1,2,0:T(8,128)(2,1)S(1)}, bf16[2,256,3,128]{3,1,2,0:T(8,128)(2,1)S(1)}, u32[]{:S(2)}, u32[]{:S(2)}) collective-permute-start(bf16[2,256,3,128]{3,1,2,0:T(8,128)(2,1)S(1)} %pad_maximum_fusion), channel_id=1, source_target_pairs={{0,88},{8,96},{16,104},{24,112},{32,120},{40,128},{48,136},{56,144... | collective-permute-start | bytes 1179656 | tf_op jit(solution)/shard_map/ppermute | solution.py:14
  244.3 104.5 %collective-permute-start.7 = (bf16[2,256,3,128]{3,1,2,0:T(8,128)(2,1)S(1)}, bf16[2,256,3,128]{3,1,2,0:T(8,128)(2,1)S(1)}, u32[]{:S(2)}, u32[]{:S(2)}) collective-permute-start(bf16[2,256,3,128]{3,1,2,0:T(8,128)(2,1)S(1)} %pad_maximum_fusion), channel_id=1, source_target_pairs={{0,96},{8,104},{16,112},{24,120},{32,128},{40,136},{48,144},{56,15... | collective-permute-start | bytes 1179656 | tf_op jit(solution)/shard_map/ppermute | solution.py:14
  259.6 94.3 %collective-permute-start.6 = (bf16[2,256,3,128]{3,1,2,0:T(8,128)(2,1)S(1)}, bf16[2,256,3,128]{3,1,2,0:T(8,128)(2,1)S(1)}, u32[]{:S(2)}, u32[]{:S(2)}) collective-permute-start(bf16[2,256,3,128]{3,1,2,0:T(8,128)(2,1)S(1)} %pad_maximum_fusion), channel_id=1, source_target_pairs={{0,104},{8,112},{16,120},{24,128},{32,136},{40,144},{48,152},{56,1... | collective-permute-start | bytes 1179656 | tf_op jit(solution)/shard_map/ppermute | solution.py:14
  279.9 85.9 %collective-permute-start.5 = (bf16[2,256,3,128]{3,1,2,0:T(8,128)(2,1)S(1)}, bf16[2,256,3,128]{3,1,2,0:T(8,128)(2,1)S(1)}, u32[]{:S(2)}, u32[]{:S(2)}) collective-permute-start(bf16[2,256,3,128]{3,1,2,0:T(8,128)(2,1)S(1)} %pad_maximum_fusion), channel_id=1, source_target_pairs={{0,120},{8,128},{16,136},{24,144},{32,152},{40,160},{48,168},{56,1... | collective-permute-start | bytes 1179656 | tf_op jit(solution)/shard_map/ppermute | solution.py:14
  298.4 78.1 %collective-permute-start.4 = (bf16[2,256,3,128]{3,1,2,0:T(8,128)(2,1)S(1)}, bf16[2,256,3,128]{3,1,2,0:T(8,128)(2,1)S(1)}, u32[]{:S(2)}, u32[]{:S(2)}) collective-permute-start(bf16[2,256,3,128]{3,1,2,0:T(8,128)(2,1)S(1)} %pad_maximum_fusion), channel_id=1, source_target_pairs={{0,128},{8,136},{16,144},{24,152},{32,160},{40,168},{48,176},{56,1... | collective-permute-start | bytes 1179656 | tf_op jit(solution)/shard_map/ppermute | solution.py:14
  329.3 48.2 %collective-permute-start.3 = (bf16[2,256,3,128]{3,1,2,0:T(8,128)(2,1)S(1)}, bf16[2,256,3,128]{3,1,2,0:T(8,128)(2,1)S(1)}, u32[]{:S(2)}, u32[]{:S(2)}) collective-permute-start(bf16[2,256,3,128]{3,1,2,0:T(8,128)(2,1)S(1)} %pad_maximum_fusion), channel_id=1, source_target_pairs={{0,136},{8,144},{16,152},{24,160},{32,168},{40,176},{48,184},{56,1... | collective-permute-start | bytes 1179656 | tf_op jit(solution)/shard_map/ppermute | solution.py:14
  449.4 393.7 %all-gather.5.cloned.1.call-start = ((), (), s32[]{:S(2)}) async-start(), calls=%async_computation.2 | async-start | bytes 4792320 | tf_op jit(solution)/shard_map/all_gather | solution.py:85
  (6 other events, 161.0 us)
Sparse Core Ops, SparseCore 0:
  449.5 84.0 all-gather.2
  535.6 307.3 all-gather.4
where the time goes:
time: 857 us; the launch traced here: 855 us
  waiting for transfers between devices  526 us (61%)
  starting transfers between devices  234 us (27%)
  matrix products  55.1 us (6%)
  other arithmetic  21.5 us (3%)
  between operations  14.1 us (2%)
    all_gather x1, waiting for transfers between devices, local(): lax.all_gather(out_weight, 'seq', axis=0, tiled=True)  310 us
    ppermute x26, starting transfers between devices, passed_along(): return lax.ppermute(array, axis, pairs)  225 us
    ppermute x26, waiting for transfers between devices, passed_along(): return lax.ppermute(array, axis, pairs)  127 us
    all_gather x1, waiting for transfers between devices, local(): all_heads = lax.all_gather(finished, 'head', axis=1, tiled=True)  83.4 us
    dot_general x27, matrix products, attend_block(): jnp.einsum('qhk,khd->qhd', weights.astype(jnp.bfloat16), kv_block[1], pre...  25.7 us
    dot_general x27, matrix products, attend_block(): jnp.einsum('qhd,khd->qhk', queries, kv_block[0], preferred_element_type=j...  24.4 us
    reduce_sum x14, other arithmetic, attend_block(): run_sum = run_sum * rescale + jnp.sum(weights, axis=-1)  20.6 us
  transfers between devices with their start and end apart: 29, of which 10 were waited for; matrix products, arithmetic and copies ran while one was open for 3% of the time, Pallas kernels for 0%

commit v1 on v0

--- a/solution.py
+++ b/solution.py
@@ -79,7 +79,8 @@
     run_max, run_sum, run_acc = softmax_state
     finished = (run_acc / run_sum[:, :, None]).astype(jnp.bfloat16)
     finished = finished.reshape(tile_rows, heads_dev * head_width)
-    all_heads = lax.all_gather(finished, "head", axis=1, tiled=True)
+    repeated = jnp.stack([finished] * lax.axis_size("head"))
+    all_heads = jnp.concatenate(lax.all_to_all(repeated, "head", 0, 0), axis=1)
     projected = jnp.dot(
         all_heads,
         lax.all_gather(out_weight, "seq", axis=0, tiled=True),

time: 857 us -> 656 us (0.77)
  the two profiles are of different devices: /device:TPU:16 before, /device:TPU:32 now
where the time goes in v1:
time: 656 us; the launch traced here: 655 us
  waiting for transfers between devices  262 us (40%)
  starting transfers between devices  225 us (34%)
  blocking collectives  73.9 us (11%)
  matrix products  53.7 us (8%)
  other arithmetic  20.8 us (3%)
  between operations  14.1 us (2%)
    ppermute x26, starting transfers between devices, passed_along(): return lax.ppermute(array, axis, pairs)  217 us
    ppermute x26, waiting for transfers between devices, passed_along(): return lax.ppermute(array, axis, pairs)  147 us
    all_gather x1, waiting for transfers between devices, local(): lax.all_gather(out_weight, 'seq', axis=0, tiled=True)  112 us
    all_to_all x1, blocking collectives, local(): all_heads = jnp.concatenate(lax.all_to_all(repeated, 'head', 0, 0), axis=1)  73.9 us
    dot_general x27, matrix products, attend_block(): jnp.einsum('qhk,khd->qhd', weights.astype(jnp.bfloat16), kv_block[1], pre...  24.9 us
    dot_general x27, matrix products, attend_block(): jnp.einsum('qhd,khd->qhk', queries, kv_block[0], preferred_element_type=j...  24.4 us
    reduce_sum x14, other arithmetic, attend_block(): run_sum = run_sum * rescale + jnp.sum(weights, axis=-1)  20.6 us
  transfers between devices with their start and end apart: 28, of which 8 were waited for; matrix products, arithmetic and copies ran while one was open for 11% of the time, Pallas kernels for 0%

profile of v1, /device:TPU:32, one launch (start us, length us, event | category | flops | bytes accessed | tf_op | source)
XLA Modules:
  0.0 654.5 jit_solution(14195702849112538360)
XLA Ops:
  16.3 8.8 %all-to-all-start = ((bf16[32,24,128]{2,0,1:T(8,128)(2,1)}), bf16[32,24,128]{2,0,1:T(8,128)(2,1)S(1)}, u32[]{:S(2)}, u32[]{:S(2)}) async-start(bf16[32,24,128]{2,0,1:T(8,128)(2,1)} %copy_bitcast_fusion), calls=%async_computation | async-start | bytes 393216 | tf_op jit(solution)/shard_map/all_to_all | solution.py:42
  27.2 2.0 all-to-all-done
  31.1 21.8 %collective-permute-done.25 = bf16[2,256,3,128]{3,1,2,0:T(8,128)(2,1)S(1)} collective-permute-done((bf16[2,256,3,128]{3,1,2,0:T(8,128)(2,1)S(1)}, bf16[2,256,3,128]{3,1,2,0:T(8,128)(2,1)S(1)}, u32[]{:S(2)}, u32[]{:S(2)}) %collective-permute-start.25) | collective-permute-done | bytes 393248 | tf_op jit(solution)/shard_map/ppermute | solution.py:14
  55.1 6.2 collective-permute-done.24
  70.1 59.2 %collective-permute-done.20 = bf16[2,256,3,128]{3,1,2,0:T(8,128)(2,1)S(1)} collective-permute-done((bf16[2,256,3,128]{3,1,2,0:T(8,128)(2,1)S(1)}, bf16[2,256,3,128]{3,1,2,0:T(8,128)(2,1)S(1)}, u32[]{:S(2)}, u32[]{:S(2)}) %collective-permute-start.20) | collective-permute-done | bytes 393248 | tf_op jit(solution)/shard_map/ppermute | solution.py:14
  136.0 4.6 collective-permute-start.12
  141.5 68.9 %collective-permute-start.11 = (bf16[2,256,3,128]{3,1,2,0:T(8,128)(2,1)S(1)}, bf16[2,256,3,128]{3,1,2,0:T(8,128)(2,1)S(1)}, u32[]{:S(2)}, u32[]{:S(2)}) collective-permute-start(bf16[2,256,3,128]{3,1,2,0:T(8,128)(2,1)S(1)} %pad_maximum_fusion), channel_id=1, source_target_pairs={{0,24},{8,32},{16,40},{24,48},{32,56},{40,64},{48,72},{56,80},{64,... | collective-permute-start | bytes 1179656 | tf_op jit(solution)/shard_map/ppermute | solution.py:14
  211.2 17.1 %collective-permute-start.10 = (bf16[2,256,3,128]{3,1,2,0:T(8,128)(2,1)S(1)}, bf16[2,256,3,128]{3,1,2,0:T(8,128)(2,1)S(1)}, u32[]{:S(2)}, u32[]{:S(2)}) collective-permute-start(bf16[2,256,3,128]{3,1,2,0:T(8,128)(2,1)S(1)} %pad_maximum_fusion), channel_id=1, source_target_pairs={{0,32},{8,40},{16,48},{24,56},{32,64},{40,72},{48,80},{56,88},{64,... | collective-permute-start | bytes 1179656 | tf_op jit(solution)/shard_map/ppermute | solution.py:14
  229.2 3.8 collective-permute-start.9
  236.1 39.0 %collective-permute-start.7 = (bf16[2,256,3,128]{3,1,2,0:T(8,128)(2,1)S(1)}, bf16[2,256,3,128]{3,1,2,0:T(8,128)(2,1)S(1)}, u32[]{:S(2)}, u32[]{:S(2)}) collective-permute-start(bf16[2,256,3,128]{3,1,2,0:T(8,128)(2,1)S(1)} %pad_maximum_fusion), channel_id=1, source_target_pairs={{0,96},{8,104},{16,112},{24,120},{32,128},{40,136},{48,144},{56,15... | collective-permute-start | bytes 1179656 | tf_op jit(solution)/shard_map/ppermute | solution.py:14
  276.1 21.0 %collective-permute-start.6 = (bf16[2,256,3,128]{3,1,2,0:T(8,128)(2,1)S(1)}, bf16[2,256,3,128]{3,1,2,0:T(8,128)(2,1)S(1)}, u32[]{:S(2)}, u32[]{:S(2)}) collective-permute-start(bf16[2,256,3,128]{3,1,2,0:T(8,128)(2,1)S(1)} %pad_maximum_fusion), channel_id=1, source_target_pairs={{0,104},{8,112},{16,120},{24,128},{32,136},{40,144},{48,152},{56,1... | collective-permute-start | bytes 1179656 | tf_op jit(solution)/shard_map/ppermute | solution.py:14
  300.3 27.2 %collective-permute-done.9 = bf16[2,256,3,128]{3,1,2,0:T(8,128)(2,1)S(1)} collective-permute-done((bf16[2,256,3,128]{3,1,2,0:T(8,128)(2,1)S(1)}, bf16[2,256,3,128]{3,1,2,0:T(8,128)(2,1)S(1)}, u32[]{:S(2)}, u32[]{:S(2)}) %collective-permute-start.9) | collective-permute-done | bytes 393248 | tf_op jit(solution)/shard_map/ppermute | solution.py:14
  329.7 20.8 %collective-permute-start.3 = (bf16[2,256,3,128]{3,1,2,0:T(8,128)(2,1)S(1)}, bf16[2,256,3,128]{3,1,2,0:T(8,128)(2,1)S(1)}, u32[]{:S(2)}, u32[]{:S(2)}) collective-permute-start(bf16[2,256,3,128]{3,1,2,0:T(8,128)(2,1)S(1)} %pad_maximum_fusion), channel_id=1, source_target_pairs={{0,136},{8,144},{16,152},{24,160},{32,168},{40,176},{48,184},{56,1... | collective-permute-start | bytes 1179656 | tf_op jit(solution)/shard_map/ppermute | solution.py:14
  353.7 17.9 %collective-permute-start.1 = (bf16[2,256,3,128]{3,1,2,0:T(8,128)(2,1)S(1)}, bf16[2,256,3,128]{3,1,2,0:T(8,128)(2,1)S(1)}, u32[]{:S(2)}, u32[]{:S(2)}) collective-permute-start(bf16[2,256,3,128]{3,1,2,0:T(8,128)(2,1)S(1)} %pad_maximum_fusion), channel_id=1, source_target_pairs={{0,160},{8,168},{16,176},{24,184},{32,192},{40,200},{48,208},{56,2... | collective-permute-start | bytes 1179656 | tf_op jit(solution)/shard_map/ppermute | solution.py:14
  372.5 23.6 %collective-permute-done.5 = bf16[2,256,3,128]{3,1,2,0:T(8,128)(2,1)S(1)} collective-permute-done((bf16[2,256,3,128]{3,1,2,0:T(8,128)(2,1)S(1)}, bf16[2,256,3,128]{3,1,2,0:T(8,128)(2,1)S(1)}, u32[]{:S(2)}, u32[]{:S(2)}) %collective-permute-start.5) | collective-permute-done | bytes 393248 | tf_op jit(solution)/shard_map/ppermute | solution.py:14
  402.2 8.9 %collective-permute-done = bf16[2,256,3,128]{3,1,2,0:T(8,128)(2,1)S(1)} collective-permute-done((bf16[2,256,3,128]{3,1,2,0:T(8,128)(2,1)S(1)}, bf16[2,256,3,128]{3,1,2,0:T(8,128)(2,1)S(1)}, u32[]{:S(2)}, u32[]{:S(2)}) %collective-permute-start) | collective-permute-done | bytes 393248 | tf_op jit(solution)/shard_map/ppermute | solution.py:14
  415.0 1.6 fusion.151
  422.6 1.5 fusion.131
  424.1 1.6 fusion.127
  425.7 1.6 fusion.123
  455.4 1.5 fusion.108
  457.0 73.9 %all_to_all.23 = bf16[8,256,384]{1,2,0:T(8,128)(2,1)S(1)} all-to-all(bf16[8,256,384]{1,2,0:T(8,128)(2,1)S(1)} %stack.7), channel_id=1, replica_groups=mesh['seq'=64,'head'=8] {'head'}, dimensions={0} | all-to-all | bytes 3145728 | tf_op jit(solution)/shard_map/all_to_all | solution.py:83
  530.9 112.3 %all-gather.2.cloned.1.call-done = bf16[3072,768]{1,0:T(8,128)(2,1)} async-done(((bf16[48,768]{1,0:T(8,128)(2,1)}), bf16[3072,768]{1,0:T(8,128)(2,1)}) %all-gather.2.cloned.1.call-update) | async-done | bytes 4718608 | tf_op jit(solution)/shard_map/all_gather | solution.py:86
  643.2 4.5 convolution_convert_fusion
  (121 shorter events, 91.2 us)
Async XLA Ops:
  10.4 50.9 %collective-permute-start.24 = (bf16[2,256,3,128]{3,1,2,0:T(8,128)(2,1)S(1)}, bf16[2,256,3,128]{3,1,2,0:T(8,128)(2,1)S(1)}, u32[]{:S(2)}, u32[]{:S(2)}) collective-permute-start(bf16[2,256,3,128]{3,1,2,0:T(8,128)(2,1)S(1)} %pad_maximum_fusion), channel_id=1, source_target_pairs={{160,0},{168,8},{176,16},{184,24},{192,32},{200,40},{208,48},{216,... | collective-permute-start | bytes 1179656 | tf_op jit(solution)/shard_map/ppermute | solution.py:14
  11.7 51.8 %collective-permute-start.23 = (bf16[2,256,3,128]{3,1,2,0:T(8,128)(2,1)S(1)}, bf16[2,256,3,128]{3,1,2,0:T(8,128)(2,1)S(1)}, u32[]{:S(2)}, u32[]{:S(2)}) collective-permute-start(bf16[2,256,3,128]{3,1,2,0:T(8,128)(2,1)S(1)} %pad_maximum_fusion), channel_id=1, source_target_pairs={{152,0},{160,8},{168,16},{176,24},{184,32},{192,40},{200,48},{208,... | collective-permute-start | bytes 1179656 | tf_op jit(solution)/shard_map/ppermute | solution.py:14
  13.0 52.7 %collective-permute-start.22 = (bf16[2,256,3,128]{3,1,2,0:T(8,128)(2,1)S(1)}, bf16[2,256,3,128]{3,1,2,0:T(8,128)(2,1)S(1)}, u32[]{:S(2)}, u32[]{:S(2)}) collective-permute-start(bf16[2,256,3,128]{3,1,2,0:T(8,128)(2,1)S(1)} %pad_maximum_fusion), channel_id=1, source_target_pairs={{136,0},{144,8},{152,16},{160,24},{168,32},{176,40},{184,48},{192,... | collective-permute-start | bytes 1179656 | tf_op jit(solution)/shard_map/ppermute | solution.py:14
  14.3 53.6 %collective-permute-start.21 = (bf16[2,256,3,128]{3,1,2,0:T(8,128)(2,1)S(1)}, bf16[2,256,3,128]{3,1,2,0:T(8,128)(2,1)S(1)}, u32[]{:S(2)}, u32[]{:S(2)}) collective-permute-start(bf16[2,256,3,128]{3,1,2,0:T(8,128)(2,1)S(1)} %pad_maximum_fusion), channel_id=1, source_target_pairs={{128,0},{136,8},{144,16},{152,24},{160,32},{168,40},{176,48},{184,... | collective-permute-start | bytes 1179656 | tf_op jit(solution)/shard_map/ppermute | solution.py:14
  25.1 618.1 %all-gather.2.cloned.1.call-start = ((), (), s32[]{:S(2)}) async-start(), calls=%async_computation.2 | async-start | bytes 4792320 | tf_op jit(solution)/shard_map/all_gather | solution.py:86
  52.9 76.5 %collective-permute-start.20 = (bf16[2,256,3,128]{3,1,2,0:T(8,128)(2,1)S(1)}, bf16[2,256,3,128]{3,1,2,0:T(8,128)(2,1)S(1)}, u32[]{:S(2)}, u32[]{:S(2)}) collective-permute-start(bf16[2,256,3,128]{3,1,2,0:T(8,128)(2,1)S(1)} %pad_maximum_fusion), channel_id=1, source_target_pairs={{120,0},{128,8},{136,16},{144,24},{152,32},{160,40},{168,48},{176,... | collective-permute-start | bytes 1179656 | tf_op jit(solution)/shard_map/ppermute | solution.py:14
  61.3 70.2 %collective-permute-start.19 = (bf16[2,256,3,128]{3,1,2,0:T(8,128)(2,1)S(1)}, bf16[2,256,3,128]{3,1,2,0:T(8,128)(2,1)S(1)}, u32[]{:S(2)}, u32[]{:S(2)}) collective-permute-start(bf16[2,256,3,128]{3,1,2,0:T(8,128)(2,1)S(1)} %pad_maximum_fusion), channel_id=1, source_target_pairs={{104,0},{112,8},{120,16},{128,24},{136,32},{144,40},{152,48},{160,... | collective-permute-start | bytes 1179656 | tf_op jit(solution)/shard_map/ppermute | solution.py:14
  63.4 70.3 %collective-permute-start.18 = (bf16[2,256,3,128]{3,1,2,0:T(8,128)(2,1)S(1)}, bf16[2,256,3,128]{3,1,2,0:T(8,128)(2,1)S(1)}, u32[]{:S(2)}, u32[]{:S(2)}) collective-permute-start(bf16[2,256,3,128]{3,1,2,0:T(8,128)(2,1)S(1)} %pad_maximum_fusion), channel_id=1, source_target_pairs={{96,0},{104,8},{112,16},{120,24},{128,32},{136,40},{144,48},{152,5... | collective-permute-start | bytes 1179656 | tf_op jit(solution)/shard_map/ppermute | solution.py:14
  65.7 70.3 %collective-permute-start.17 = (bf16[2,256,3,128]{3,1,2,0:T(8,128)(2,1)S(1)}, bf16[2,256,3,128]{3,1,2,0:T(8,128)(2,1)S(1)}, u32[]{:S(2)}, u32[]{:S(2)}) collective-permute-start(bf16[2,256,3,128]{3,1,2,0:T(8,128)(2,1)S(1)} %pad_maximum_fusion), channel_id=1, source_target_pairs={{88,0},{96,8},{104,16},{112,24},{120,32},{128,40},{136,48},{144,56... | collective-permute-start | bytes 1179656 | tf_op jit(solution)/shard_map/ppermute | solution.py:14
  67.9 73.6 %collective-permute-start.16 = (bf16[2,256,3,128]{3,1,2,0:T(8,128)(2,1)S(1)}, bf16[2,256,3,128]{3,1,2,0:T(8,128)(2,1)S(1)}, u32[]{:S(2)}, u32[]{:S(2)}) collective-permute-start(bf16[2,256,3,128]{3,1,2,0:T(8,128)(2,1)S(1)} %pad_maximum_fusion), channel_id=1, source_target_pairs={{40,0},{48,8},{56,16},{64,24},{72,32},{80,40},{88,48},{96,56},{104... | collective-permute-start | bytes 1179656 | tf_op jit(solution)/shard_map/ppermute | solution.py:14
  129.3 81.9 %collective-permute-start.15 = (bf16[2,256,3,128]{3,1,2,0:T(8,128)(2,1)S(1)}, bf16[2,256,3,128]{3,1,2,0:T(8,128)(2,1)S(1)}, u32[]{:S(2)}, u32[]{:S(2)}) collective-permute-start(bf16[2,256,3,128]{3,1,2,0:T(8,128)(2,1)S(1)} %pad_maximum_fusion), channel_id=1, source_target_pairs={{32,0},{40,8},{48,16},{56,24},{64,32},{72,40},{80,48},{88,56},{96,... | collective-permute-start | bytes 1179656 | tf_op jit(solution)/shard_map/ppermute | solution.py:14
  131.5 97.6 %collective-permute-start.14 = (bf16[2,256,3,128]{3,1,2,0:T(8,128)(2,1)S(1)}, bf16[2,256,3,128]{3,1,2,0:T(8,128)(2,1)S(1)}, u32[]{:S(2)}, u32[]{:S(2)}) collective-permute-start(bf16[2,256,3,128]{3,1,2,0:T(8,128)(2,1)S(1)} %pad_maximum_fusion), channel_id=1, source_target_pairs={{24,0},{32,8},{40,16},{48,24},{56,32},{64,40},{72,48},{80,56},{88,... | collective-permute-start | bytes 1179656 | tf_op jit(solution)/shard_map/ppermute | solution.py:14
  133.8 100.2 %collective-permute-start.13 = (bf16[2,256,3,128]{3,1,2,0:T(8,128)(2,1)S(1)}, bf16[2,256,3,128]{3,1,2,0:T(8,128)(2,1)S(1)}, u32[]{:S(2)}, u32[]{:S(2)}) collective-permute-start(bf16[2,256,3,128]{3,1,2,0:T(8,128)(2,1)S(1)} %pad_maximum_fusion), channel_id=1, source_target_pairs={{8,0},{16,8},{24,16},{32,24},{40,32},{48,40},{56,48},{64,56},{72,6... | collective-permute-start | bytes 1179656 | tf_op jit(solution)/shard_map/ppermute | solution.py:14
  136.0 100.2 %collective-permute-start.12 = (bf16[2,256,3,128]{3,1,2,0:T(8,128)(2,1)S(1)}, bf16[2,256,3,128]{3,1,2,0:T(8,128)(2,1)S(1)}, u32[]{:S(2)}, u32[]{:S(2)}) collective-permute-start(bf16[2,256,3,128]{3,1,2,0:T(8,128)(2,1)S(1)} %pad_maximum_fusion), channel_id=1, source_target_pairs={{0,8},{8,16},{16,24},{24,32},{32,40},{40,48},{48,56},{56,64},{64,7... | collective-permute-start | bytes 1179656 | tf_op jit(solution)/shard_map/ppermute | solution.py:14
  141.5 134.6 %collective-permute-start.11 = (bf16[2,256,3,128]{3,1,2,0:T(8,128)(2,1)S(1)}, bf16[2,256,3,128]{3,1,2,0:T(8,128)(2,1)S(1)}, u32[]{:S(2)}, u32[]{:S(2)}) collective-permute-start(bf16[2,256,3,128]{3,1,2,0:T(8,128)(2,1)S(1)} %pad_maximum_fusion), channel_id=1, source_target_pairs={{0,24},{8,32},{16,40},{24,48},{32,56},{40,64},{48,72},{56,80},{64,... | collective-permute-start | bytes 1179656 | tf_op jit(solution)/shard_map/ppermute | solution.py:14
  211.2 86.9 %collective-permute-start.10 = (bf16[2,256,3,128]{3,1,2,0:T(8,128)(2,1)S(1)}, bf16[2,256,3,128]{3,1,2,0:T(8,128)(2,1)S(1)}, u32[]{:S(2)}, u32[]{:S(2)}) collective-permute-start(bf16[2,256,3,128]{3,1,2,0:T(8,128)(2,1)S(1)} %pad_maximum_fusion), channel_id=1, source_target_pairs={{0,32},{8,40},{16,48},{24,56},{32,64},{40,72},{48,80},{56,88},{64,... | collective-permute-start | bytes 1179656 | tf_op jit(solution)/shard_map/ppermute | solution.py:14
  229.2 98.3 %collective-permute-start.9 = (bf16[2,256,3,128]{3,1,2,0:T(8,128)(2,1)S(1)}, bf16[2,256,3,128]{3,1,2,0:T(8,128)(2,1)S(1)}, u32[]{:S(2)}, u32[]{:S(2)}) collective-permute-start(bf16[2,256,3,128]{3,1,2,0:T(8,128)(2,1)S(1)} %pad_maximum_fusion), channel_id=1, source_target_pairs={{0,40},{8,48},{16,56},{24,64},{32,72},{40,80},{48,88},{56,96},{64,... | collective-permute-start | bytes 1179656 | tf_op jit(solution)/shard_map/ppermute | solution.py:14
  234.0 95.7 %collective-permute-start.8 = (bf16[2,256,3,128]{3,1,2,0:T(8,128)(2,1)S(1)}, bf16[2,256,3,128]{3,1,2,0:T(8,128)(2,1)S(1)}, u32[]{:S(2)}, u32[]{:S(2)}) collective-permute-start(bf16[2,256,3,128]{3,1,2,0:T(8,128)(2,1)S(1)} %pad_maximum_fusion), channel_id=1, source_target_pairs={{0,88},{8,96},{16,104},{24,112},{32,120},{40,128},{48,136},{56,144... | collective-permute-start | bytes 1179656 | tf_op jit(solution)/shard_map/ppermute | solution.py:14
  236.1 115.3 %collective-permute-start.7 = (bf16[2,256,3,128]{3,1,2,0:T(8,128)(2,1)S(1)}, bf16[2,256,3,128]{3,1,2,0:T(8,128)(2,1)S(1)}, u32[]{:S(2)}, u32[]{:S(2)}) collective-permute-start(bf16[2,256,3,128]{3,1,2,0:T(8,128)(2,1)S(1)} %pad_maximum_fusion), channel_id=1, source_target_pairs={{0,96},{8,104},{16,112},{24,120},{32,128},{40,136},{48,144},{56,15... | collective-permute-start | bytes 1179656 | tf_op jit(solution)/shard_map/ppermute | solution.py:14
  276.1 77.6 %collective-permute-start.6 = (bf16[2,256,3,128]{3,1,2,0:T(8,128)(2,1)S(1)}, bf16[2,256,3,128]{3,1,2,0:T(8,128)(2,1)S(1)}, u32[]{:S(2)}, u32[]{:S(2)}) collective-permute-start(bf16[2,256,3,128]{3,1,2,0:T(8,128)(2,1)S(1)} %pad_maximum_fusion), channel_id=1, source_target_pairs={{0,104},{8,112},{16,120},{24,128},{32,136},{40,144},{48,152},{56,1... | collective-permute-start | bytes 1179656 | tf_op jit(solution)/shard_map/ppermute | solution.py:14
  298.1 98.1 %collective-permute-start.5 = (bf16[2,256,3,128]{3,1,2,0:T(8,128)(2,1)S(1)}, bf16[2,256,3,128]{3,1,2,0:T(8,128)(2,1)S(1)}, u32[]{:S(2)}, u32[]{:S(2)}) collective-permute-start(bf16[2,256,3,128]{3,1,2,0:T(8,128)(2,1)S(1)} %pad_maximum_fusion), channel_id=1, source_target_pairs={{0,120},{8,128},{16,136},{24,144},{32,152},{40,160},{48,168},{56,1... | collective-permute-start | bytes 1179656 | tf_op jit(solution)/shard_map/ppermute | solution.py:14
  327.5 71.0 %collective-permute-start.4 = (bf16[2,256,3,128]{3,1,2,0:T(8,128)(2,1)S(1)}, bf16[2,256,3,128]{3,1,2,0:T(8,128)(2,1)S(1)}, u32[]{:S(2)}, u32[]{:S(2)}) collective-permute-start(bf16[2,256,3,128]{3,1,2,0:T(8,128)(2,1)S(1)} %pad_maximum_fusion), channel_id=1, source_target_pairs={{0,128},{8,136},{16,144},{24,152},{32,160},{40,168},{48,176},{56,1... | collective-permute-start | bytes 1179656 | tf_op jit(solution)/shard_map/ppermute | solution.py:14
  329.7 69.7 %collective-permute-start.3 = (bf16[2,256,3,128]{3,1,2,0:T(8,128)(2,1)S(1)}, bf16[2,256,3,128]{3,1,2,0:T(8,128)(2,1)S(1)}, u32[]{:S(2)}, u32[]{:S(2)}) collective-permute-start(bf16[2,256,3,128]{3,1,2,0:T(8,128)(2,1)S(1)} %pad_maximum_fusion), channel_id=1, source_target_pairs={{0,136},{8,144},{16,152},{24,160},{32,168},{40,176},{48,184},{56,1... | collective-permute-start | bytes 1179656 | tf_op jit(solution)/shard_map/ppermute | solution.py:14
  351.5 48.9 %collective-permute-start.2 = (bf16[2,256,3,128]{3,1,2,0:T(8,128)(2,1)S(1)}, bf16[2,256,3,128]{3,1,2,0:T(8,128)(2,1)S(1)}, u32[]{:S(2)}, u32[]{:S(2)}) collective-permute-start(bf16[2,256,3,128]{3,1,2,0:T(8,128)(2,1)S(1)} %pad_maximum_fusion), channel_id=1, source_target_pairs={{0,152},{8,160},{16,168},{24,176},{32,184},{40,192},{48,200},{56,2... | collective-permute-start | bytes 1179656 | tf_op jit(solution)/shard_map/ppermute | solution.py:14
  (6 other events, 147.5 us)
Sparse Core Ops, SparseCore 0:
  28.0 615.1 all-gather.1
